TPU v7x, 512 devices: a whole 4x8x8 slice. The times are simulated.
512 devices in a mesh: dp: 16 (over z_hi, x), expert: 32 (over z_lo, y, core).
Axes of the slice: x: 4, y: 8, z: 8 (z_hi: 4, z_lo: 2; z = z_hi * 2 + z_lo), core: 2. Of those that a mesh axis runs over, the one named last changes fastest.
Arguments:
- tokens: bfloat16 [6144, 6144], P('expert', 'dp'), may hold values from -6 to 6
- expert_of: int32 [6144], P('expert'), may hold values from 0 to 31, as said below
- router_weight: float32 [6144], P('expert'), may hold values from 0.2 to 1
- cotangent: bfloat16 [6144, 6144], P('expert', 'dp'), may hold values from -6 to 6
- gate_up_weight: bfloat16 [32, 2, 6144, 1024], P('expert', None, 'dp'), may hold values from -0.078125 to 0.078125
- down_weight: bfloat16 [32, 1024, 6144], P('expert', None, 'dp'), may hold values from -0.1875 to 0.1875
Outputs:
- layer_out: bfloat16 [6144, 6144], P('expert', 'dp')
- grad_tokens: bfloat16 [6144, 6144], P('expert', 'dp')
- grad_gate_up: bfloat16 [32, 2, 6144, 1024], P('expert', None, 'dp')
- grad_down: bfloat16 [32, 1024, 6144], P('expert', None, 'dp')
Inputs may be any that keep to these rules, and one draw needn't show every extreme that they name: `expert_of`: take the tokens in aligned blocks of 192, one block for each index of expert. One expert, the same for all blocks, is named by exactly 12 tokens of every block; every other expert is named by at most 9 tokens of a block, and in every block some other expert by exactly 9.
All inputs are finite; a program needn't handle non-finite values.
Results may differ from a plain program's by a relative error of at most 0.0058.
Values may be sent and summed in bfloat16 or wider, within the bound.
No kernel may reach another device: no remote copies, remote signals or barrier semaphores. Data moves between devices by JAX's collectives and lax.ppermute only.
A program may use at most 64 MiB of HBM per device.

v0:
```python
import jax
import jax.numpy as jnp
from jax import lax
from jax.sharding import Mesh, PartitionSpec as P

NX = 4
NZ = 4
TOKEN_AXES = ("zl", "y", "core")


def slots_of(expert_of, width, room):
    count = expert_of.shape[0]
    index = jnp.arange(count, dtype=jnp.int32)
    earlier = (expert_of[:, None] == expert_of[None, :]) & (index[None, :] < index[:, None])
    position = jnp.sum(earlier.astype(jnp.int32), axis=1)
    slot = expert_of * room + position
    return (slot[None, :] == jnp.arange(width, dtype=jnp.int32)[:, None]).astype(jnp.bfloat16)


def dot(a, b, dims):
    return lax.dot_general(a, b, (dims, ((), ())), preferred_element_type=jnp.float32)


def sum_blocks(blocks):
    b = [blocks[i].astype(jnp.float32) for i in range(blocks.shape[0])]
    return b[0] + b[1] + (b[2] + b[3])


def scatter_sum(partial):
    rows, width = partial.shape
    first = lax.all_to_all(partial.reshape(NX, rows // NX, width), "x", 0, 0, tiled=True)
    first = sum_blocks(first).astype(jnp.bfloat16)
    second = lax.all_to_all(first.reshape(NZ, rows // NX // NZ, width), "zh", 0, 0, tiled=True)
    return sum_blocks(second)


def gather_rows(part):
    return lax.all_gather(lax.all_gather(part, "zh", axis=0, tiled=True), "x", axis=0, tiled=True)


def shards(tokens, expert_of, router_weight, cotangent, gate_up_weight, down_weight):
    tok, feat = tokens.shape
    experts = 32
    room = 2 * tok // experts
    rows = experts * room
    w_gate = gate_up_weight[0, 0]
    w_up = gate_up_weight[0, 1]
    w_down = down_weight[0]
    ff = w_gate.shape[1]
    scaled = (router_weight[:, None] * cotangent.astype(jnp.float32)).astype(jnp.bfloat16)
    dispatch = slots_of(expert_of, rows, room)
    send = jnp.concatenate(
        [dot(dispatch, tokens, ((1,), (0,))), dot(dispatch, scaled, ((1,), (0,)))], axis=1
    ).astype(jnp.bfloat16)
    recv = lax.all_to_all(
        send.reshape(experts, room, 2 * feat), TOKEN_AXES, 0, 0, tiled=True
    ).reshape(rows, 2 * feat)
    x_rows = recv[:, :feat]
    s_rows = recv[:, feat:]
    partial = jnp.concatenate(
        [
            dot(x_rows, w_gate, ((1,), (0,))).astype(jnp.bfloat16),
            dot(x_rows, w_up, ((1,), (0,))).astype(jnp.bfloat16),
            dot(s_rows, w_down, ((1,), (1,))).astype(jnp.bfloat16),
        ],
        axis=1,
    )
    total = scatter_sum(partial)
    gate = total[:, :ff]
    up = total[:, ff : 2 * ff]
    hidden_grad = total[:, 2 * ff :]
    sig = jax.nn.sigmoid(gate)
    act = gate * sig
    part = jnp.concatenate(
        [act * up, hidden_grad * up * sig * (1.0 + gate * (1.0 - sig)), hidden_grad * act], axis=1
    ).astype(jnp.bfloat16)
    full = gather_rows(part)
    hidden = full[:, :ff]
    gate_grad = full[:, ff : 2 * ff]
    up_grad = full[:, 2 * ff :]
    expert_out = dot(hidden, w_down, ((1,), (0,)))
    row_grad = dot(gate_grad, w_gate, ((1,), (1,))) + dot(up_grad, w_up, ((1,), (1,)))
    back = jnp.concatenate([expert_out, row_grad], axis=1).astype(jnp.bfloat16)
    back = lax.all_to_all(
        back.reshape(experts, room, 2 * feat), TOKEN_AXES, 0, 0, tiled=True
    ).reshape(rows, 2 * feat)
    grad_gate = dot(x_rows, gate_grad, ((0,), (0,)))
    grad_up = dot(x_rows, up_grad, ((0,), (0,)))
    grad_down = dot(hidden, s_rows, ((0,), (0,)))
    out = dot(dispatch, back, ((0,), (0,)))
    layer_out = (router_weight[:, None] * out[:, :feat]).astype(jnp.bfloat16)
    grad_tokens = out[:, feat:].astype(jnp.bfloat16)
    return (
        layer_out,
        grad_tokens,
        jnp.stack([grad_gate, grad_up]).astype(jnp.bfloat16)[None],
        grad_down.astype(jnp.bfloat16)[None],
    )


def solution(mesh):
    fine = Mesh(mesh.devices.reshape(NZ, NX, 2, 8, 2), ("zh", "x", "zl", "y", "core"))
    dp = ("zh", "x")
    ex = TOKEN_AXES
    return jax.shard_map(
        shards,
        mesh=fine,
        in_specs=(P(ex, dp), P(ex), P(ex), P(ex, dp), P(ex, None, dp, None), P(ex, None, dp)),
        out_specs=(P(ex, dp), P(ex, dp), P(ex, None, dp, None), P(ex, None, dp)),
        check_vma=False,
    )
```

profile of v0, /device:TPU:8, one launch (start us, length us, event | category | flops | bytes accessed | tf_op | source)
XLA Modules:
  0.0 203.6 jit_solution(1716345662355274634)
XLA Ops:
  7.2 0.9 convert_reduce_fusion
  8.2 0.7 multiply_add_fusion
  8.9 1.3 convolution_convert_fusion.7
  10.2 1.2 convolution_convert_fusion.8
  11.5 0.1 pad_maximum_fusion.2
  11.5 32.7 %all_to_all.20 = bf16[32,12,768]{2,1,0:T(8,128)(2,1)S(1)} all-to-all(bf16[32,12,768]{2,1,0:T(8,128)(2,1)S(1)} %pad_maximum_fusion.2), channel_id=1, replica_groups=mesh['zh'=4,'x'=4,'zl'=2,'y'=8,'core'=2] {'zl','y','core'}, dimensions={0} | all-to-all | bytes 1179648 | tf_op jit(solution)/shard_map/all_to_all | solution.py:55
  44.2 0.1 reshape.84
  44.4 1.8 convolution_convert_fusion.4
  46.2 0.6 convolution_convert_fusion.5
  46.8 0.6 convolution_convert_fusion.3
  47.4 0.2 pad_maximum_fusion
  47.6 32.9 %all_to_all.21 = bf16[4,96,3072]{2,1,0:T(8,128)(2,1)S(1)} all-to-all(bf16[4,96,3072]{2,1,0:T(8,128)(2,1)S(1)} %bitcast.28), channel_id=1, replica_groups=mesh['zh'=4,'x'=4,'zl'=2,'y'=8,'core'=2] {'x'}, dimensions={0} | all-to-all | bytes 4718592 | tf_op jit(solution)/shard_map/all_to_all | solution.py:31
  80.5 0.3 add_convert_fusion
  80.8 25.2 %all_to_all.22 = bf16[4,24,3072]{2,1,0:T(8,128)(2,1)S(1)} all-to-all(bf16[4,24,3072]{2,1,0:T(8,128)(2,1)S(1)} %bitcast.29), channel_id=1, replica_groups=mesh['zh'=4,'x'=4,'zl'=2,'y'=8,'core'=2] {'zh'}, dimensions={0} | all-to-all | bytes 1179648 | tf_op jit(solution)/shard_map/all_to_all | solution.py:33
  106.2 15.8 %all_gather.6 = bf16[96,3072]{1,0:T(8,128)(2,1)} all-gather(bf16[24,3072]{1,0:T(8,128)(2,1)S(1)} %pad_maximum_fusion.4), channel_id=1, replica_groups=mesh['zh'=4,'x'=4,'zl'=2,'y'=8,'core'=2] {'zh'}, dimensions={0}, use_global_device_ids=true | all-gather | bytes 737280 | tf_op jit(solution)/shard_map/all_gather | solution.py:38
  121.9 34.1 %all-gather.2.cloned.1.call-done = bf16[384,3072]{1,0:T(8,128)(2,1)} async-done(((bf16[96,3072]{1,0:T(8,128)(2,1)}), bf16[384,3072]{1,0:T(8,128)(2,1)}) %all-gather.2.cloned.1.call-update) | async-done | bytes 2359312 | tf_op jit(solution)/shard_map/all_gather | solution.py:38
  156.0 1.7 fusion.8
  157.8 1.7 fusion.3
  159.7 1.2 slice.94
  160.8 0.2 dot_general.43
  161.0 0.6 convolution_convert_fusion.6
  161.7 1.2 copy.18
  162.9 8.5 %all-to-all-start.3 = ((bf16[32,12,768]{2,1,0:T(8,128)(2,1)}), bf16[32,12,768]{2,1,0:T(8,128)(2,1)S(1)}, u32[]{:S(2)}, u32[]{:S(2)}) async-start(bf16[32,12,768]{2,1,0:T(8,128)(2,1)} %copy.18), calls=%async_computation.3 | async-start | bytes 1572864 | tf_op jit(solution)/shard_map/all_to_all | solution.py:84
  171.5 1.7 fusion
  173.2 1.7 fusion.1
  174.9 1.3 pad_maximum_fusion.1
  176.2 2.7 %fusion.2 = bf16[1,1024,384]{2,1,0:T(8,128)(2,1)} fusion(bf16[384,768]{1,0:T(8,128)(2,1)S(1)} %reshape.84, bf16[384,3072]{1,0:T(8,128)(2,1)} %all-gather.2.cloned.1.call-done), kind=kOutput, calls=%fused_computation.10 | convolution fusion | flops 302383104 | bytes 1867776 | tf_op jit(solution)/shard_map/dot_general | solution.py:21
  178.9 15.9 %all-to-all-done.3 = bf16[32,12,768]{2,1,0:T(8,128)(2,1)S(1)} async-done(((bf16[32,12,768]{2,1,0:T(8,128)(2,1)}), bf16[32,12,768]{2,1,0:T(8,128)(2,1)S(1)}, u32[]{:S(2)}, u32[]{:S(2)}) %all-to-all-start.3) | async-done | bytes 589856 | tf_op jit(solution)/shard_map/all_to_all | solution.py:84
  194.8 0.1 reshape.86
  195.0 0.4 fusion.20
  195.4 0.7 slice.159
  196.0 0.8 fusion.21
  (16 shorter events, 0.5 us)
Async XLA Ops:
  7.2 39.6 %copy-start = (bf16[1,1024,384]{2,1,0:T(8,128)(2,1)S(1)}, bf16[1,1024,384]{2,1,0:T(8,128)(2,1)}, u32[]{:S(2)}) copy-start(bf16[1,1024,384]{2,1,0:T(8,128)(2,1)} %param.11) | copy-start | bytes 2359300
  7.2 148.8 %all-gather.2.cloned.1.call-start = ((), (), s32[]{:S(2)}) async-start(), calls=%async_computation.4 | async-start | bytes 2949120 | tf_op jit(solution)/shard_map/all_gather | solution.py:38
  44.4 1.8 copy-start.2
  162.9 31.9 %all-to-all-start.3 = ((bf16[32,12,768]{2,1,0:T(8,128)(2,1)}), bf16[32,12,768]{2,1,0:T(8,128)(2,1)S(1)}, u32[]{:S(2)}, u32[]{:S(2)}) async-start(bf16[32,12,768]{2,1,0:T(8,128)(2,1)} %copy.18), calls=%async_computation.3 | async-start | bytes 1572864 | tf_op jit(solution)/shard_map/all_to_all | solution.py:84
  178.9 17.1 %copy-start.1 = (f32[192]{0:T(256)S(1)}, f32[192]{0:T(256)}, u32[]{:S(2)}) copy-start(f32[192]{0:T(256)} %param.8) | copy-start | bytes 2308
Sparse Core Ops, SparseCore 0:
  122.1 33.9 all-gather.1
where the time goes:
time: 204 us
  blocking collectives  107 us (52%)
  waiting for transfers between devices  50 us (25%)
  matrix products  16.1 us (8%)
  between operations  14.2 us (7%)
  starting transfers between devices  8.55 us (4%)
  other arithmetic  4.44 us (2%)
  local copies, waits for them, and re-layouts  3.8 us (2%)
    all_gather x1, waiting for transfers between devices, gather_rows(): lax.all_gather(lax.all_gather(part, 'zh', axis=0, tiled=True), 'x', axis=...  34.1 us
    all_to_all x1, blocking collectives, scatter_sum(): lax.all_to_all(partial.reshape(NX, rows // NX, width), 'x', 0, 0, tiled=T...  32.9 us
    all_to_all x1, blocking collectives, shards(): lax.all_to_all(send.reshape(experts, room, 2 * feat), TOKEN_AXES, 0, 0, t...  32.7 us
    all_to_all x1, blocking collectives, scatter_sum(): lax.all_to_all(first.reshape(NZ, rows // NX // NZ, width), 'zh', 0, 0, ti...  25.2 us
    dot_general x12, matrix products, dot(): lax.dot_general(a, b, (dims, ((), ())), preferred_element_type=jnp.float32)  16.1 us
    all_to_all x1, waiting for transfers between devices, shards(): lax.all_to_all(back.reshape(experts, room, 2 * feat), TOKEN_AXES, 0, 0, t...  15.9 us
    all_gather x1, blocking collectives, gather_rows(): lax.all_gather(part, 'zh', axis=0, tiled=True)  15.8 us
    all_to_all x1, starting transfers between devices, shards(): lax.all_to_all(back.reshape(experts, room, 2 * feat), TOKEN_AXES, 0, 0, t...  8.51 us
  transfers between devices with their start and end apart: 2, of which 2 were waited for; matrix products, arithmetic and copies ran while one was open for 4% of the time, Pallas kernels for 0%

commit v1 on v0

--- a/solution.py
+++ b/solution.py
@@ -1,3 +1,4 @@
+import functools
 import jax
 import jax.numpy as jnp
 from jax import lax
@@ -6,6 +7,18 @@
 NX = 4
 NZ = 4
 TOKEN_AXES = ("zl", "y", "core")
+
+
+def run_regions_on(field, dev_axis):
+    history = []
+    for _ in range(lax.axis_size(dev_axis)):
+        history.append(field)
+    after = lax.all_to_all(jnp.stack(history), dev_axis, 0, 0)
+    raw_out = jnp.concatenate(after, axis=0)
+    return raw_out
+
+
+handle_the_results = functools.partial(run_regions_on, dev_axis="x")
 
 
 def slots_of(expert_of, width, room):
@@ -35,7 +48,7 @@
 
 
 def gather_rows(part):
-    return lax.all_gather(lax.all_gather(part, "zh", axis=0, tiled=True), "x", axis=0, tiled=True)
+    return handle_the_results(lax.all_gather(part, "zh", axis=0, tiled=True))
 
 
 def shards(tokens, expert_of, router_weight, cotangent, gate_up_weight, down_weight):

time: 204 us -> 187 us (0.917)
  waiting for transfers between devices: 50 us -> 18.3 us
  blocking collectives: 107 us -> 136 us
  between operations: 14.2 us -> 0.88 us
  local copies, waits for them, and re-layouts: 3.8 us -> 8.55 us
  starting transfers between devices: 8.55 us -> 4.6 us
  matrix products: 16.1 us -> 13.5 us
    all_gather x1 -> x0, waiting for transfers between devices: 34.1 us -> none  [gather_rows(): lax.all_gather(lax.all_gather(part, 'zh', axis=0, tiled=True), 'x', axis=...]
    all_to_all x0 -> x1, blocking collectives: none -> 30.2 us  [run_regions_on(): after = lax.all_to_all(jnp.stack(history), dev_axis, 0, 0)]
    all_to_all x1, starting transfers between devices: 8.51 us -> 4.6 us  [shards(): lax.all_to_all(back.reshape(experts, room, 2 * feat), TOKEN_AXES, 0, 0, t...]
    dot_general x12, matrix products: 16.1 us -> 13.5 us  [dot(): lax.dot_general(a, b, (dims, ((), ())), preferred_element_type=jnp.float32)]
    all_to_all x1, waiting for transfers between devices: 15.9 us -> 18.3 us  [shards(): lax.all_to_all(back.reshape(experts, room, 2 * feat), TOKEN_AXES, 0, 0, t...]
  transfers between devices with their start and end apart: 2 -> 1, of which waited for: 2 -> 1; matrix products, arithmetic and copies ran while one was open for 4% -> 3% of each run, Pallas kernels for 0% -> 0%
where the time goes in v1:
time: 187 us; the launch traced here: 186 us
  blocking collectives  136 us (73%)
  waiting for transfers between devices  18.3 us (10%)
  matrix products  13.5 us (7%)
  local copies, waits for them, and re-layouts  8.55 us (5%)
  starting transfers between devices  4.6 us (2%)
  other arithmetic  4.45 us (2%)
    all_to_all x1, blocking collectives, scatter_sum(): lax.all_to_all(partial.reshape(NX, rows // NX, width), 'x', 0, 0, tiled=T...  32.9 us
    all_to_all x1, blocking collectives, shards(): lax.all_to_all(send.reshape(experts, room, 2 * feat), TOKEN_AXES, 0, 0, t...  32.7 us
    all_to_all x1, blocking collectives, run_regions_on(): after = lax.all_to_all(jnp.stack(history), dev_axis, 0, 0)  30.2 us
    all_to_all x1, blocking collectives, scatter_sum(): lax.all_to_all(first.reshape(NZ, rows // NX // NZ, width), 'zh', 0, 0, ti...  25.2 us
    all_to_all x1, waiting for transfers between devices, shards(): lax.all_to_all(back.reshape(experts, room, 2 * feat), TOKEN_AXES, 0, 0, t...  18.3 us
    all_gather x1, blocking collectives, gather_rows(): return handle_the_results(lax.all_gather(part, 'zh', axis=0, tiled=True))  15 us
    dot_general x12, matrix products, dot(): lax.dot_general(a, b, (dims, ((), ())), preferred_element_type=jnp.float32)  13.5 us
    all_to_all x1, starting transfers between devices, shards(): lax.all_to_all(back.reshape(experts, room, 2 * feat), TOKEN_AXES, 0, 0, t...  4.6 us
  transfers between devices with their start and end apart: 1, of which 1 were waited for; matrix products, arithmetic and copies ran while one was open for 3% of the time, Pallas kernels for 0%

profile of v1, /device:TPU:8, one launch (start us, length us, event | category | flops | bytes accessed | tf_op | source)
XLA Modules:
  0.0 186.3 jit_solution(5914491448121782317)
XLA Ops:
  0.6 0.9 convert_reduce_fusion
  1.6 0.7 multiply_add_fusion
  2.3 1.3 convolution_convert_fusion.7
  3.6 1.2 convolution_convert_fusion.8
  5.0 32.7 %all_to_all.25 = bf16[32,12,768]{2,1,0:T(8,128)(2,1)S(1)} all-to-all(bf16[32,12,768]{2,1,0:T(8,128)(2,1)S(1)} %pad_maximum_fusion.2), channel_id=1, replica_groups=mesh['zh'=4,'x'=4,'zl'=2,'y'=8,'core'=2] {'zl','y','core'}, dimensions={0} | all-to-all | bytes 1179648 | tf_op jit(solution)/shard_map/all_to_all | solution.py:68
  37.8 1.9 %convolution_convert_fusion.4 = bf16[384,1024]{1,0:T(8,128)(2,1)S(1)} fusion(bf16[1,2,384,1024]{3,2,1,0:T(8,128)(2,1)} %param.10, bf16[384,768]{1,0:T(8,128)(2,1)S(1)} %reshape.89), kind=kOutput, calls=%fused_computation.6 | convolution fusion | flops 302383104 | bytes 1867776 | tf_op jit(solution)/shard_map/dot_general | solution.py:34
  39.8 0.6 convolution_convert_fusion.5
  40.4 0.6 convolution_convert_fusion.3
  41.1 32.9 %all_to_all.26 = bf16[4,96,3072]{2,1,0:T(8,128)(2,1)S(1)} all-to-all(bf16[4,96,3072]{2,1,0:T(8,128)(2,1)S(1)} %bitcast.29), channel_id=1, replica_groups=mesh['zh'=4,'x'=4,'zl'=2,'y'=8,'core'=2] {'x'}, dimensions={0} | all-to-all | bytes 4718592 | tf_op jit(solution)/shard_map/all_to_all | solution.py:44
  74.0 0.3 add_convert_fusion
  74.4 25.2 %all_to_all.27 = bf16[4,24,3072]{2,1,0:T(8,128)(2,1)S(1)} all-to-all(bf16[4,24,3072]{2,1,0:T(8,128)(2,1)S(1)} %bitcast.36), channel_id=1, replica_groups=mesh['zh'=4,'x'=4,'zl'=2,'y'=8,'core'=2] {'zh'}, dimensions={0} | all-to-all | bytes 1179648 | tf_op jit(solution)/shard_map/all_to_all | solution.py:46
  99.7 15.0 %all_gather.3 = bf16[96,3072]{1,0:T(8,128)(2,1)S(1)} all-gather(bf16[24,3072]{1,0:T(8,128)(2,1)S(1)} %pad_maximum_fusion.4), channel_id=1, replica_groups=mesh['zh'=4,'x'=4,'zl'=2,'y'=8,'core'=2] {'zh'}, dimensions={0}, use_global_device_ids=true | all-gather | bytes 737280 | tf_op jit(solution)/shard_map/all_gather | solution.py:51
  114.7 0.3 stack.16
  115.0 30.2 %all_to_all.28 = bf16[4,96,3072]{2,1,0:T(8,128)(2,1)S(1)} all-to-all(bf16[4,96,3072]{2,1,0:T(8,128)(2,1)S(1)} %stack.16), channel_id=1, replica_groups=mesh['zh'=4,'x'=4,'zl'=2,'y'=8,'core'=2] {'x'}, dimensions={0} | all-to-all | bytes 4718592 | tf_op jit(solution)/shard_map/all_to_all | solution.py:16
  145.2 0.6 fusion.8
  145.8 0.9 slice.94
  146.7 1.3 fusion.3
  148.0 1.0 concatenate.36
  149.1 0.8 copy.17
  149.8 2.1 %dot_general.43 = bf16[32,12,1024]{2,1,0:T(8,128)(2,1)} reshape(bf16[384,1024]{1,0:T(8,128)(2,1)} %slice.94) | data formatting | bytes 1572864 | tf_op jit(solution)/shard_map/dot_general | solution.py:34
  151.9 1.9 %convolution_convert_fusion.6 = bf16[32,12,384]{2,0,1:T(8,128)(2,1)S(1)} fusion(bf16[1,1024,384]{2,1,0:T(8,128)(2,1)S(1)} %copy-done, bf16[32,12,1024]{2,1,0:T(8,128)(2,1)} %dot_general.43), kind=kOutput, calls=%fused_computation.13 | convolution fusion | flops 302137344 | bytes 1867776 | tf_op jit(solution)/shard_map/dot_general | solution.py:34
  153.9 1.2 copy.18
  155.1 4.6 %all-to-all-start.4 = ((bf16[32,12,768]{2,1,0:T(8,128)(2,1)}), bf16[32,12,768]{2,1,0:T(8,128)(2,1)}, u32[]{:S(2)}, u32[]{:S(2)}) async-start(bf16[32,12,768]{2,1,0:T(8,128)(2,1)} %copy.18), calls=%async_computation.4 | async-start | bytes 1572864 | tf_op jit(solution)/shard_map/all_to_all | solution.py:97
  159.7 1.6 fusion
  161.4 0.6 fusion.1
  162.0 1.3 pad_maximum_fusion.1
  163.3 1.6 fusion.2
  164.8 18.3 %all-to-all-done.4 = bf16[32,12,768]{2,1,0:T(8,128)(2,1)} async-done(((bf16[32,12,768]{2,1,0:T(8,128)(2,1)}), bf16[32,12,768]{2,1,0:T(8,128)(2,1)}, u32[]{:S(2)}, u32[]{:S(2)}) %all-to-all-start.4) | async-done | bytes 589856 | tf_op jit(solution)/shard_map/all_to_all | solution.py:97
  183.2 1.3 reshape.92
  184.4 0.4 fusion.20
  184.8 0.7 slice.159
  185.5 0.8 fusion.21
  (21 shorter events, 0.7 us)
Async XLA Ops:
  0.6 39.7 %copy-start = (bf16[1,1024,384]{2,1,0:T(8,128)(2,1)S(1)}, bf16[1,1024,384]{2,1,0:T(8,128)(2,1)}, u32[]{:S(2)}) copy-start(bf16[1,1024,384]{2,1,0:T(8,128)(2,1)} %param.11) | copy-start | bytes 2359300
  37.8 2.6 %copy-start.1 = (bf16[384,768]{1,0:T(8,128)(2,1)}, bf16[384,768]{1,0:T(8,128)(2,1)S(1)}, u32[]{:S(2)}) copy-start(bf16[384,768]{1,0:T(8,128)(2,1)S(1)} %reshape.89) | copy-start | bytes 1769476
  37.8 2.0 %copy-start.5 = (bf16[1,2,384,1024]{3,2,1,0:T(8,128)(2,1)S(1)}, bf16[1,2,384,1024]{3,2,1,0:T(8,128)(2,1)}, u32[]{:S(2)}) copy-start(bf16[1,2,384,1024]{3,2,1,0:T(8,128)(2,1)} %param.10) | copy-start | bytes 4718596
  151.9 1.9 %copy-start.3 = (bf16[32,12,384]{2,0,1:T(8,128)(2,1)S(1)}, bf16[32,12,384]{2,0,1:T(8,128)(2,1)}, u32[]{:S(2)}) copy-start(bf16[32,12,384]{2,0,1:T(8,128)(2,1)} %copy.17) | copy-start | bytes 884740
  155.1 28.0 %all-to-all-start.4 = ((bf16[32,12,768]{2,1,0:T(8,128)(2,1)}), bf16[32,12,768]{2,1,0:T(8,128)(2,1)}, u32[]{:S(2)}, u32[]{:S(2)}) async-start(bf16[32,12,768]{2,1,0:T(8,128)(2,1)} %copy.18), calls=%async_computation.4 | async-start | bytes 1572864 | tf_op jit(solution)/shard_map/all_to_all | solution.py:97
  159.7 1.6 copy-start.2
  164.8 20.7 %copy-start.4 = (f32[192]{0:T(256)S(1)}, f32[192]{0:T(256)}, u32[]{:S(2)}) copy-start(f32[192]{0:T(256)} %param.8) | copy-start | bytes 2308
